TPU v7x, 128 devices: a whole 4x4x4 slice. The times are simulated.
128 devices in a mesh: gx: 16 (over x, y), gy: 8 (over z, core).
Axes of the slice: x: 4, y: 4, z: 4, core: 2. Of those that a mesh axis runs over, the one named last changes fastest.
Arguments:
- plume_field: bfloat16 [2, 20, 128, 128, 16, 128], P(None, None, 'gx', 'gy'), may hold values from -6 to 6
- mode_weights: bfloat16 [24, 20, 20, 16, 2, 288], P('gy', None, None, 'gx'), may hold values from -1 to 1
Outputs:
- spectral_mix: float32 [2, 24, 20, 16, 2, 288], P(None, 'gy', None, 'gx')
All inputs are finite; a program needn't handle non-finite values.
Results may differ from a plain program's by a relative error of at most 0.003.
Values sent between devices are 32-bit elements; how exact they have to be, the bound alone decides.
A program may use at most 192 MiB of HBM per device.

v0:
```python
import math

import jax
import jax.numpy as jnp
from jax import lax
from jax.sharding import PartitionSpec as P

GRID_X = 128
GRID_Y = 128
GRID_Z = 128
STEPS_T = 16
MODES_X = 24
MODES_Y = 24
MODES_Z = 24
MODES_T = 8
HALF_Z = 12


def kept_modes(kept_count, axis_length):
    position = jnp.arange(kept_count, dtype=jnp.int32)
    return jnp.where(position < kept_count // 2, position, axis_length - kept_count + position)


def plane_table():
    moments = jnp.arange(STEPS_T, dtype=jnp.int32)
    depths = jnp.arange(GRID_Z, dtype=jnp.int32)
    time_freq = jnp.arange(MODES_T, dtype=jnp.int32)
    depth_freq = kept_modes(MODES_Z, GRID_Z).reshape(2, HALF_Z)
    phase_index = (
        time_freq[None, None, :, None, None]
        * moments[:, None, None, None, None]
        * (GRID_Z // STEPS_T)
        + depth_freq[None, None, None, :, :] * depths[None, :, None, None, None]
    ) % GRID_Z
    phases = 2.0 * math.pi / GRID_Z * phase_index.astype(jnp.float32)
    factor = 1.0 / math.sqrt(STEPS_T * GRID_Z)
    twiddle = jnp.stack([factor * jnp.cos(phases), -factor * jnp.sin(phases)], axis=4)
    return twiddle.reshape(STEPS_T, GRID_Z, 2 * MODES_T * MODES_Z).astype(jnp.bfloat16)


def line_parts(kept_count, axis_length):
    frequency = kept_modes(kept_count, axis_length)
    positions = jnp.arange(axis_length, dtype=jnp.int32)
    phase_index = frequency[:, None] * positions[None, :] % axis_length
    phases = 2.0 * math.pi / axis_length * phase_index.astype(jnp.float32)
    factor = 1.0 / math.sqrt(axis_length)
    return factor * jnp.cos(phases), factor * jnp.sin(phases)


def line_matrix(kept_count, axis_length):
    frequency = kept_modes(kept_count, axis_length)
    positions = jnp.arange(axis_length, dtype=jnp.int32)
    phase_index = frequency[:, None] * positions[None, :] % axis_length
    phases = 2.0 * math.pi / axis_length * phase_index.astype(jnp.float32)
    factor = 1.0 / math.sqrt(axis_length)
    cosines = factor * jnp.cos(phases)
    sines = factor * jnp.sin(phases)
    upper = jnp.stack([cosines, sines], axis=1)
    lower = jnp.stack([-sines, cosines], axis=1)
    return jnp.stack([upper, lower], axis=0)


def one_sample(moved, mode_weights, kron, second):
    high = lax.Precision.HIGH
    pairs, parts_x, _, lanes = moved.shape
    parts_y = second.shape[0]
    rows_y = second.shape[1] // 2
    kept_here = MODES_X // parts_y

    moved = moved.reshape(pairs, parts_x * 2, HALF_Z, lanes)
    upper = moved.astype(jnp.bfloat16)
    lower = (moved - upper.astype(jnp.float32)).astype(jnp.bfloat16)
    numbers = (((1, 2), (1, 3)), ((), ()))
    after_x = lax.dot_general(kron, upper, numbers, preferred_element_type=jnp.float32) + lax.dot_general(
        kron, lower, numbers, preferred_element_type=jnp.float32
    )
    after_x = after_x.reshape(parts_y, kept_here * 2 * rows_y, pairs * HALF_Z)
    gathered = lax.all_to_all(after_x, "gy", 0, 0, tiled=False)
    gathered = gathered.reshape(parts_y, kept_here, 2 * rows_y, pairs * HALF_Z)

    after_y = lax.dot_general(gathered, second, (((0, 2), (0, 1)), ((1,), (2,))), precision=high)
    after_y = after_y.reshape(kept_here, pairs, HALF_Z, 2, MODES_Y)
    after_y = jnp.transpose(after_y, (0, 1, 3, 2, 4))
    after_y = after_y.reshape(kept_here, pairs, 2, HALF_Z * MODES_Y)

    real_part = after_y[:, :, None, 0]
    imag_part = after_y[:, :, None, 1]
    weight_re = mode_weights[:, :, :, 0, 0].astype(jnp.float32)
    weight_im = mode_weights[:, :, :, 0, 1].astype(jnp.float32)
    mixed_re = jnp.sum(real_part * weight_re - imag_part * weight_im, axis=1)
    mixed_im = jnp.sum(real_part * weight_im + imag_part * weight_re, axis=1)
    return jnp.stack([mixed_re, mixed_im], axis=2)[:, :, None]


def local(plume_field, mode_weights):
    samples, channels, rows_x, rows_y = plume_field.shape[:4]
    parts_x = GRID_X // rows_x
    parts_y = GRID_Y // rows_y
    groups = 2 * MODES_T
    per_group = 2 * HALF_Z
    kept_here = MODES_X // parts_y
    lanes = rows_x * rows_y
    pairs = samples * channels

    twiddle = plane_table()
    field = plume_field.reshape(pairs, lanes, STEPS_T, GRID_Z)
    spectrum = jnp.einsum("tzn,Bxtz->Bnx", twiddle, field, preferred_element_type=jnp.float32)
    spectrum = spectrum.reshape(samples, channels, groups, per_group, lanes)

    first = line_matrix(MODES_X, GRID_X).reshape(2, parts_y, kept_here, 2, parts_x, rows_x)
    first = jnp.transpose(first, (1, 2, 0, 4, 3, 5)).reshape(MODES_X * 2, parts_x * 2, rows_x)
    lane = jnp.arange(lanes, dtype=jnp.int32)
    spread = (lane[None, :] // rows_y == jnp.arange(rows_x, dtype=jnp.int32)[:, None]).astype(jnp.float32)
    keep = (lane[None, :] % rows_y == jnp.arange(rows_y, dtype=jnp.int32)[:, None]).astype(jnp.float32)
    spread_first = jnp.einsum("aip,pq->aiq", first, spread, precision=lax.Precision.HIGHEST)
    kron = spread_first[:, None] * keep[None, :, None, :]
    kron = kron.reshape(MODES_X * 2 * rows_y, parts_x * 2, lanes).astype(jnp.bfloat16)

    second = line_matrix(MODES_Y, GRID_Y).reshape(2, MODES_Y, 2, parts_y, rows_y)
    second = jnp.transpose(second, (3, 2, 4, 0, 1)).reshape(parts_y, 2 * rows_y, 1, 2 * MODES_Y)
    second = jnp.broadcast_to(second, (parts_y, 2 * rows_y, kept_here, 2 * MODES_Y))

    chunks = [spectrum[sample] for sample in range(samples)]
    kron, chunks[1:] = lax.optimization_barrier((kron, chunks[1:]))
    outs = []
    for sample in range(samples):
        moved = lax.all_to_all(chunks[sample], "gx", 1, 1, tiled=False)
        outs.append(one_sample(moved, mode_weights, kron, second))
    return jnp.stack(outs, axis=0)


def solution(mesh):
    return jax.shard_map(
        local,
        mesh=mesh,
        in_specs=(P(None, None, "gx", "gy", None, None), P("gy", None, None, "gx", None, None)),
        out_specs=P(None, "gy", None, "gx", None, None),
        check_vma=False,
    )
```

profile of v0, /device:TPU:1, one launch (start us, length us, event | category | flops | bytes accessed | tf_op | source)
XLA Modules:
  0.0 198.6 jit_solution(17821811943980497492)
XLA Ops:
  0.1 6.7 %multiply_convert_fusion.1 = (bf16[16,128,8,2,1,12]{1,0,5,4,3,2:T(8,128)(2,1)S(1)}, bf16[16,128,8,2,1,12]{1,0,5,4,3,2:T(8,128)(2,1)S(1)}) fusion(s32[128,2,12]{0,2,1:T(8,128)S(1)} %iota_multiply_fusion, s32[16,8]{0,1:T(8,128)S(1)} %multiply_multiply_fusion), kind=kLoop, calls=%fused_computation.45 | loop fusion | flops 7077888 | bytes 1585664 | tf_op jit(solution)/shard_map/convert.2
  6.9 12.1 %fusion.11 = f32[40,384,128]{2,1,0:T(8,128)S(1)} fusion(bf16[40,128,16,128]{3,2,1,0:T(8,128)(2,1)} %bitcast.127, bf16[16,128,384]{1,0,2:T(8,128)(2,1)S(1)} %bitcast.126), kind=kOutput, calls=%fused_computation.24 | convolution fusion | flops 8053063680 | bytes 30408704 | tf_op jit(solution)/shard_map/tzn,Bxtz->Bnx/dot_general | solution.py:107
  19.0 2.7 %fusion.61 = (f32[20,384,128]{2,1,0:T(8,128)}, f32[20,384,128]{2,1,0:T(8,128)S(1)}) fusion(f32[40,384,128]{2,1,0:T(8,128)S(1)} %fusion.11), kind=kLoop, calls=%fused_computation.108 | loop fusion | bytes 15728640 | tf_op jit(solution)/shard_map/slice | solution.py:123
  21.7 2.3 %copy.81 = f32[20,16,24,128]{3,2,0,1:T(8,128)} copy(f32[20,16,24,128]{3,2,1,0:T(8,128)S(1)} %bitcast.113) | data formatting | bytes 7864320 | tf_op jit(solution)/shard_map/squeeze | solution.py:123
  23.9 7.6 %all-to-all-start = ((f32[20,16,24,128]{3,2,0,1:T(8,128)}), f32[20,16,24,128]{3,2,0,1:T(8,128)}, u32[]{:S(2)}, u32[]{:S(2)}) async-start(f32[20,16,24,128]{3,2,0,1:T(8,128)} %copy.81), calls=%async_computation | async-start | bytes 7864320 | tf_op jit(solution)/shard_map/all_to_all | solution.py:127
  32.7 1.0 fusion.45
  33.7 4.3 %fusion.2 = bf16[768,32,128]{2,0,1:T(8,128)(2,1)} fusion(f32[768,128]{1,0:T(8,128)S(1)} %bitcast.125, f32[48,32,128]{2,0,1:T(8,128)S(1)} %fusion.45), kind=kLoop, calls=%fused_computation.3 | loop fusion | flops 6291456 | bytes 7471104 | tf_op jit(solution)/shard_map/convert_element_type | solution.py:117
  38.0 2.4 %copy.92 = f32[20,16,24,128]{3,2,0,1:T(8,128)} copy(f32[20,16,24,128]{3,2,1,0:T(8,128)S(1)} %bitcast.112) | data formatting | bytes 7864320 | tf_op jit(solution)/shard_map/optimization_barrier | solution.py:124
  40.4 3.8 %fusion.62 = (bf16[3,20,20,1,1,288]{5,4,3,2,1,0:T(2,128)(2,1)S(1)}, bf16[3,20,20,1,1,288]{5,4,3,2,1,0:T(2,128)(2,1)}) fusion(bf16[3,20,20,1,2,288]{5,4,3,2,1,0:T(2,128)(2,1)S(1)} %copy-done.1), kind=kLoop, calls=%fused_computation.109 | loop fusion | bytes 2764800 | tf_op jit(solution)/shard_map/slice | solution.py:89
  44.2 42.8 %all-to-all-done = f32[20,16,24,128]{3,2,0,1:T(8,128)} async-done(((f32[20,16,24,128]{3,2,0,1:T(8,128)}), f32[20,16,24,128]{3,2,0,1:T(8,128)}, u32[]{:S(2)}, u32[]{:S(2)}) %all-to-all-start) | async-done | bytes 3932192 | tf_op jit(solution)/shard_map/all_to_all | solution.py:127
  87.0 11.4 %all-to-all-start.2 = ((f32[20,16,24,128]{3,2,0,1:T(8,128)}), f32[20,16,24,128]{3,2,0,1:T(8,128)}, u32[]{:S(2)}, u32[]{:S(2)}) async-start(f32[20,16,24,128]{3,2,0,1:T(8,128)} %copy.92), calls=%async_computation.2 | async-start | bytes 7864320 | tf_op jit(solution)/shard_map/all_to_all | solution.py:127
  98.4 3.0 %copy.82 = f32[20,16,24,128]{3,0,2,1:T(8,128)S(1)} copy(f32[20,16,24,128]{3,2,0,1:T(8,128)} %all-to-all-done) | data formatting | bytes 7864320 | tf_op jit(solution)/shard_map/all_to_all | solution.py:127
  101.4 5.1 %fusion.27 = f32[768,20,12]{0,1,2:T(8,128)S(1)} fusion(f32[20,32,12,128]{3,0,2,1:T(8,128)S(1)} %bitcast.120, bf16[768,32,128]{2,0,1:T(8,128)(2,1)} %fusion.2), kind=kOutput, calls=%fused_computation.46 | convolution fusion | flops 1509949440 | bytes 10960896 | tf_op jit(solution)/shard_map/dot_general | solution.py:74
  106.5 2.2 %fusion.42 = f32[768,20,12]{0,1,2:T(8,128)S(1)} fusion(f32[768,20,12]{0,1,2:T(8,128)S(1)} %fusion.27, f32[20,32,12,128]{3,0,2,1:T(8,128)S(1)} %bitcast.121, bf16[768,32,128]{2,0,1:T(8,128)(2,1)S(1)} %bitcast.115), kind=kOutput, calls=%fused_computation.51 | convolution fusion | flops 1514065920 | bytes 11698176 | tf_op jit(solution)/shard_map/dot_general | solution.py:74
  108.9 1.4 reshape.423
  110.3 2.4 %copy.86 = f32[8,96,240]{2,1,0:T(8,128)} copy(f32[8,96,240]{1,0,2:T(8,128)} %reshape.423) | data formatting | bytes 1474560 | tf_op jit(solution)/shard_map/reshape | solution.py:77
  112.7 33.9 %all-to-all-done.2 = f32[20,16,24,128]{3,2,0,1:T(8,128)} async-done(((f32[20,16,24,128]{3,2,0,1:T(8,128)}), f32[20,16,24,128]{3,2,0,1:T(8,128)}, u32[]{:S(2)}, u32[]{:S(2)}) %all-to-all-start.2) | async-done | bytes 3932192 | tf_op jit(solution)/shard_map/all_to_all | solution.py:127
  146.6 10.4 %all-to-all-start.1 = ((f32[8,96,240]{2,1,0:T(8,128)}), f32[8,96,240]{2,1,0:T(8,128)}, u32[]{:S(2)}, u32[]{:S(2)}) async-start(f32[8,96,240]{2,1,0:T(8,128)} %copy.86), calls=%async_computation.1 | async-start | bytes 1572864 | tf_op jit(solution)/shard_map/all_to_all | solution.py:78
  157.1 3.0 %copy.93 = f32[20,16,24,128]{3,0,2,1:T(8,128)S(1)} copy(f32[20,16,24,128]{3,2,0,1:T(8,128)} %all-to-all-done.2) | data formatting | bytes 7864320 | tf_op jit(solution)/shard_map/all_to_all | solution.py:127
  160.1 5.1 %fusion.33 = f32[768,20,12]{0,1,2:T(8,128)S(1)} fusion(f32[20,32,12,128]{3,0,2,1:T(8,128)S(1)} %bitcast.118, bf16[768,32,128]{2,0,1:T(8,128)(2,1)} %fusion.2), kind=kOutput, calls=%fused_computation.48 | convolution fusion | flops 1509949440 | bytes 10960896 | tf_op jit(solution)/shard_map/dot_general | solution.py:74
  165.2 2.2 %fusion.39 = f32[768,20,12]{0,1,2:T(8,128)S(1)} fusion(f32[768,20,12]{0,1,2:T(8,128)S(1)} %fusion.33, f32[20,32,12,128]{3,0,2,1:T(8,128)S(1)} %bitcast.119, bf16[768,32,128]{2,0,1:T(8,128)(2,1)S(1)} %bitcast.117), kind=kOutput, calls=%fused_computation.50 | convolution fusion | flops 1514065920 | bytes 11698176 | tf_op jit(solution)/shard_map/dot_general | solution.py:74
  167.6 1.4 reshape.428
  169.0 2.5 %copy.97 = f32[8,96,240]{2,1,0:T(8,128)} copy(f32[8,96,240]{1,0,2:T(8,128)} %reshape.428) | data formatting | bytes 1474560 | tf_op jit(solution)/shard_map/reshape | solution.py:77
  171.5 4.8 %all-to-all-start.3 = ((f32[8,96,240]{2,1,0:T(8,128)}), f32[8,96,240]{2,1,0:T(8,128)}, u32[]{:S(2)}, u32[]{:S(2)}) async-start(f32[8,96,240]{2,1,0:T(8,128)} %copy.97), calls=%async_computation.3 | async-start | bytes 1572864 | tf_op jit(solution)/shard_map/all_to_all | solution.py:78
  177.1 2.0 convolution_bitcast_fusion.1
  179.1 1.3 reshape.425
  180.4 1.2 copy.89
  182.3 6.3 %all-to-all-done.3 = f32[8,96,240]{2,1,0:T(8,128)} async-done(((f32[8,96,240]{2,1,0:T(8,128)}), f32[8,96,240]{2,1,0:T(8,128)}, u32[]{:S(2)}, u32[]{:S(2)}) %all-to-all-start.3) | async-done | bytes 737312 | tf_op jit(solution)/shard_map/all_to_all | solution.py:78
  188.6 2.0 convolution_bitcast_fusion
  190.5 1.3 reshape.430
  191.9 1.2 copy.99
  193.8 3.1 %fusion.15 = (f32[3,20,288]{2,1,0:T(8,128)S(1)}, f32[3,20,288]{2,1,0:T(8,128)S(1)}, f32[3,20,288]{2,1,0:T(8,128)S(1)}, f32[3,20,288]{2,1,0:T(8,128)S(1)}) fusion(f32[3,20,288]{2,1,0:T(8,128)S(1)} %get-tuple-element.31, f32[3,20,288]{2,1,0:T(8,128)S(1)} %get-tuple-element.32, bf16[3,20,20,1,1,288]{5,4,3,2,1,0:T(2,128)(2,1)} %get-tuple-element.18, ...), kind=kLoop, calls=%fused_computation.31 | loop fusion | flops 6151680 | bytes 1935360 | tf_op jit(solution)/shard_map/reduce_sum | solution.py:90
  (49 shorter events, 5.5 us)
Async XLA Ops:
  23.9 63.0 %all-to-all-start = ((f32[20,16,24,128]{3,2,0,1:T(8,128)}), f32[20,16,24,128]{3,2,0,1:T(8,128)}, u32[]{:S(2)}, u32[]{:S(2)}) async-start(f32[20,16,24,128]{3,2,0,1:T(8,128)} %copy.81), calls=%async_computation | async-start | bytes 7864320 | tf_op jit(solution)/shard_map/all_to_all | solution.py:127
  33.7 4.3 %copy-start = (f32[20,384,128]{2,1,0:T(8,128)S(1)}, f32[20,384,128]{2,1,0:T(8,128)}, u32[]{:S(2)}) copy-start(f32[20,384,128]{2,1,0:T(8,128)} %get-tuple-element.15) | copy-start | bytes 11796484
  38.0 2.4 %copy-start.1 = (bf16[3,20,20,1,2,288]{5,4,3,2,1,0:T(2,128)(2,1)S(1)}, bf16[3,20,20,1,2,288]{5,4,3,2,1,0:T(2,128)(2,1)}, u32[]{:S(2)}) copy-start(bf16[3,20,20,1,2,288]{5,4,3,2,1,0:T(2,128)(2,1)} %param.3) | copy-start | bytes 4147204
  87.0 59.7 %all-to-all-start.2 = ((f32[20,16,24,128]{3,2,0,1:T(8,128)}), f32[20,16,24,128]{3,2,0,1:T(8,128)}, u32[]{:S(2)}, u32[]{:S(2)}) async-start(f32[20,16,24,128]{3,2,0,1:T(8,128)} %copy.92), calls=%async_computation.2 | async-start | bytes 7864320 | tf_op jit(solution)/shard_map/all_to_all | solution.py:127
  98.3 8.1 %slice-start = ((s8[6291456]{0:T(1024)(128)(4,1)}), s8[4194304]{0:T(1024)(128)(4,1)S(1)}, s32[]{:S(2)}) async-start(s8[6291456]{0:T(1024)(128)(4,1)} %bitcast.114), calls=%async_computation.4 | async-start | bytes 8388608
  101.4 5.1 %slice-start.1 = ((s8[6291456]{0:T(1024)(128)(4,1)}), s8[2097152]{0:T(1024)(128)(4,1)S(1)}, s32[]{:S(2)}) async-start(s8[6291456]{0:T(1024)(128)(4,1)} %bitcast.114), calls=%async_computation.5 | async-start | bytes 4194304
  146.6 24.9 %all-to-all-start.1 = ((f32[8,96,240]{2,1,0:T(8,128)}), f32[8,96,240]{2,1,0:T(8,128)}, u32[]{:S(2)}, u32[]{:S(2)}) async-start(f32[8,96,240]{2,1,0:T(8,128)} %copy.86), calls=%async_computation.1 | async-start | bytes 1572864 | tf_op jit(solution)/shard_map/all_to_all | solution.py:78
  157.1 8.1 %slice-start.2 = ((s8[6291456]{0:T(1024)(128)(4,1)}), s8[4194304]{0:T(1024)(128)(4,1)S(1)}, s32[]{:S(2)}) async-start(s8[6291456]{0:T(1024)(128)(4,1)} %bitcast.116), calls=%async_computation.6 | async-start | bytes 8388608
  160.1 5.1 %slice-start.3 = ((s8[6291456]{0:T(1024)(128)(4,1)}), s8[2097152]{0:T(1024)(128)(4,1)S(1)}, s32[]{:S(2)}) async-start(s8[6291456]{0:T(1024)(128)(4,1)} %bitcast.116), calls=%async_computation.7 | async-start | bytes 4194304
  171.5 17.1 %all-to-all-start.3 = ((f32[8,96,240]{2,1,0:T(8,128)}), f32[8,96,240]{2,1,0:T(8,128)}, u32[]{:S(2)}, u32[]{:S(2)}) async-start(f32[8,96,240]{2,1,0:T(8,128)} %copy.97), calls=%async_computation.3 | async-start | bytes 1572864 | tf_op jit(solution)/shard_map/all_to_all | solution.py:78
where the time goes:
time: 199 us
  waiting for transfers between devices  83 us (42%)
  starting transfers between devices  34.2 us (17%)
  local copies, waits for them, and re-layouts  33.1 us (17%)
  matrix products  31.4 us (16%)
  other arithmetic  16.5 us (8%)
    all_to_all x2, waiting for transfers between devices, local(): moved = lax.all_to_all(chunks[sample], 'gx', 1, 1, tiled=False)  76.7 us
    all_to_all x2, starting transfers between devices, local(): moved = lax.all_to_all(chunks[sample], 'gx', 1, 1, tiled=False)  19 us
    all_to_all x2, starting transfers between devices, one_sample(): gathered = lax.all_to_all(after_x, 'gy', 0, 0, tiled=False)  15.2 us
    dot_general x1, matrix products, local(): jnp.einsum('tzn,Bxtz->Bnx', twiddle, field, preferred_element_type=jnp.fl...  12.1 us
    dot_general x2, matrix products, one_sample(): lax.dot_general(kron, upper, numbers, preferred_element_type=jnp.float32)  10.2 us
    reshape x4, local copies, waits for them, and re-layouts, one_sample(): after_x = after_x.reshape(parts_y, kept_here * 2 * rows_y, pairs * HALF_Z)  7.69 us
    another operation x1, other arithmetic  6.65 us
    all_to_all x2, waiting for transfers between devices, one_sample(): gathered = lax.all_to_all(after_x, 'gy', 0, 0, tiled=False)  6.27 us
  transfers between devices with their start and end apart: 4, of which 3 were waited for; matrix products, arithmetic and copies ran while one was open for 24% of the time, Pallas kernels for 0%

commit v1 on v0

--- a/solution.py
+++ b/solution.py
@@ -71,8 +71,11 @@
     upper = moved.astype(jnp.bfloat16)
     lower = (moved - upper.astype(jnp.float32)).astype(jnp.bfloat16)
     numbers = (((1, 2), (1, 3)), ((), ()))
-    after_x = lax.dot_general(kron, upper, numbers, preferred_element_type=jnp.float32) + lax.dot_general(
-        kron, lower, numbers, preferred_element_type=jnp.float32
+    kron_upper, kron_lower = kron
+    after_x = (
+        lax.dot_general(kron_upper, upper, numbers, preferred_element_type=jnp.float32)
+        + lax.dot_general(kron_upper, lower, numbers, preferred_element_type=jnp.float32)
+        + lax.dot_general(kron_lower, upper, numbers, preferred_element_type=jnp.float32)
     )
     after_x = after_x.reshape(parts_y, kept_here * 2 * rows_y, pairs * HALF_Z)
     gathered = lax.all_to_all(after_x, "gy", 0, 0, tiled=False)
@@ -114,7 +117,9 @@
     keep = (lane[None, :] % rows_y == jnp.arange(rows_y, dtype=jnp.int32)[:, None]).astype(jnp.float32)
     spread_first = jnp.einsum("aip,pq->aiq", first, spread, precision=lax.Precision.HIGHEST)
     kron = spread_first[:, None] * keep[None, :, None, :]
-    kron = kron.reshape(MODES_X * 2 * rows_y, parts_x * 2, lanes).astype(jnp.bfloat16)
+    kron = kron.reshape(MODES_X * 2 * rows_y, parts_x * 2, lanes)
+    kron_upper = kron.astype(jnp.bfloat16)
+    kron = (kron_upper, (kron - kron_upper.astype(jnp.float32)).astype(jnp.bfloat16))
 
     second = line_matrix(MODES_Y, GRID_Y).reshape(2, MODES_Y, 2, parts_y, rows_y)
     second = jnp.transpose(second, (3, 2, 4, 0, 1)).reshape(parts_y, 2 * rows_y, 1, 2 * MODES_Y)

time: 199 us -> 202 us (1.015)
  waiting for transfers between devices: 83 us -> 77.2 us
  matrix products: 31.4 us -> 36.2 us
  other arithmetic: 16.5 us -> 20.1 us
    all_to_all x2, waiting for transfers between devices: 76.7 us -> 70.9 us  [local(): moved = lax.all_to_all(chunks[sample], 'gx', 1, 1, tiled=False)]
    dot_general x4 -> x6, matrix products: 14.5 us -> 19.2 us  [the longest x2 10.6 us: one_sample(): lax.dot_general(kron_upper, upper, numbers, preferred_element_type=jnp.fl...]
    convert_element_type x1, other arithmetic: 4.31 us -> 7.84 us  [local(): (kron - kron_upper.astype(jnp.float32)).astype(jnp.bfloat16)]
  transfers between devices with their start and end apart: 4 -> 4, of which waited for: 3 -> 3; matrix products, arithmetic and copies ran while one was open for 24% -> 28% of each run, Pallas kernels for 0% -> 0%
where the time goes in v1:
time: 202 us; the launch traced here: 201 us
  waiting for transfers between devices  77.2 us (38%)
  matrix products  36.2 us (18%)
  starting transfers between devices  34.2 us (17%)
  local copies, waits for them, and re-layouts  33 us (16%)
  other arithmetic  20.1 us (10%)
    all_to_all x2, waiting for transfers between devices, local(): moved = lax.all_to_all(chunks[sample], 'gx', 1, 1, tiled=False)  70.9 us
    all_to_all x2, starting transfers between devices, local(): moved = lax.all_to_all(chunks[sample], 'gx', 1, 1, tiled=False)  19 us
    all_to_all x2, starting transfers between devices, one_sample(): gathered = lax.all_to_all(after_x, 'gy', 0, 0, tiled=False)  15.2 us
    dot_general x1, matrix products, local(): jnp.einsum('tzn,Bxtz->Bnx', twiddle, field, preferred_element_type=jnp.fl...  12.1 us
    dot_general x2, matrix products, one_sample(): lax.dot_general(kron_upper, upper, numbers, preferred_element_type=jnp.fl...  10.6 us
    convert_element_type x1, other arithmetic, local(): (kron - kron_upper.astype(jnp.float32)).astype(jnp.bfloat16)  7.84 us
    reshape x4, local copies, waits for them, and re-layouts, one_sample(): after_x = after_x.reshape(parts_y, kept_here * 2 * rows_y, pairs * HALF_Z)  7.7 us
    another operation x1, other arithmetic  6.65 us
  transfers between devices with their start and end apart: 4, of which 3 were waited for; matrix products, arithmetic and copies ran while one was open for 28% of the time, Pallas kernels for 0%

profile of v1, /device:TPU:1, one launch (start us, length us, event | category | flops | bytes accessed | tf_op | source)
XLA Modules:
  0.0 201.1 jit_solution(12775637657656056531)
XLA Ops:
  0.1 6.7 %multiply_convert_fusion.1 = (bf16[16,128,8,2,1,12]{1,0,5,4,3,2:T(8,128)(2,1)S(1)}, bf16[16,128,8,2,1,12]{1,0,5,4,3,2:T(8,128)(2,1)S(1)}) fusion(s32[128,2,12]{0,2,1:T(8,128)S(1)} %iota_multiply_fusion, s32[16,8]{0,1:T(8,128)S(1)} %multiply_multiply_fusion), kind=kLoop, calls=%fused_computation.51 | loop fusion | flops 7077888 | bytes 1585664 | tf_op jit(solution)/shard_map/convert.2
  6.9 12.1 %fusion.17 = f32[40,384,128]{2,1,0:T(8,128)S(1)} fusion(bf16[40,128,16,128]{3,2,1,0:T(8,128)(2,1)} %bitcast.162, bf16[16,128,384]{1,0,2:T(8,128)(2,1)S(1)} %bitcast.160), kind=kOutput, calls=%fused_computation.30 | convolution fusion | flops 8053063680 | bytes 30408704 | tf_op jit(solution)/shard_map/tzn,Bxtz->Bnx/dot_general | solution.py:110
  19.0 2.6 %fusion.79 = (f32[20,384,128]{2,1,0:T(8,128)}, f32[20,384,128]{2,1,0:T(8,128)S(1)}) fusion(f32[40,384,128]{2,1,0:T(8,128)S(1)} %fusion.17), kind=kLoop, calls=%fused_computation.118 | loop fusion | bytes 15728640 | tf_op jit(solution)/shard_map/slice | solution.py:128
  21.6 2.3 %copy.81 = f32[20,16,24,128]{3,2,0,1:T(8,128)} copy(f32[20,16,24,128]{3,2,1,0:T(8,128)S(1)} %bitcast.142) | data formatting | bytes 7864320 | tf_op jit(solution)/shard_map/squeeze | solution.py:128
  23.8 7.6 %all-to-all-start = ((f32[20,16,24,128]{3,2,0,1:T(8,128)}), f32[20,16,24,128]{3,2,0,1:T(8,128)}, u32[]{:S(2)}, u32[]{:S(2)}) async-start(f32[20,16,24,128]{3,2,0,1:T(8,128)} %copy.81), calls=%async_computation | async-start | bytes 7864320 | tf_op jit(solution)/shard_map/all_to_all | solution.py:132
  33.6 7.8 %fusion.4 = (bf16[768,32,128]{2,0,1:T(8,128)(2,1)}, bf16[768,32,128]{2,0,1:T(8,128)(2,1)}) fusion(f32[768,128]{1,0:T(8,128)S(1)} %bitcast.161, f32[48,32,128]{2,0,1:T(8,128)S(1)} %fusion.63), kind=kLoop, calls=%fused_computation.5 | loop fusion | flops 15728640 | bytes 13762560 | tf_op jit(solution)/shard_map/convert_element_type | solution.py:122
  41.5 2.3 %copy.92 = f32[20,16,24,128]{3,2,0,1:T(8,128)} copy(f32[20,16,24,128]{3,2,1,0:T(8,128)S(1)} %bitcast.141) | data formatting | bytes 7864320 | tf_op jit(solution)/shard_map/optimization_barrier | solution.py:129
  43.7 3.9 %fusion.80 = (bf16[3,20,20,1,1,288]{5,4,3,2,1,0:T(2,128)(2,1)S(1)}, bf16[3,20,20,1,1,288]{5,4,3,2,1,0:T(2,128)(2,1)}) fusion(bf16[3,20,20,1,2,288]{5,4,3,2,1,0:T(2,128)(2,1)S(1)} %copy-done.1), kind=kLoop, calls=%fused_computation.119 | loop fusion | bytes 2764800 | tf_op jit(solution)/shard_map/slice | solution.py:92
  47.6 39.2 %all-to-all-done = f32[20,16,24,128]{3,2,0,1:T(8,128)} async-done(((f32[20,16,24,128]{3,2,0,1:T(8,128)}), f32[20,16,24,128]{3,2,0,1:T(8,128)}, u32[]{:S(2)}, u32[]{:S(2)}) %all-to-all-start) | async-done | bytes 3932192 | tf_op jit(solution)/shard_map/all_to_all | solution.py:132
  86.9 11.4 %all-to-all-start.2 = ((f32[20,16,24,128]{3,2,0,1:T(8,128)}), f32[20,16,24,128]{3,2,0,1:T(8,128)}, u32[]{:S(2)}, u32[]{:S(2)}) async-start(f32[20,16,24,128]{3,2,0,1:T(8,128)} %copy.92), calls=%async_computation.2 | async-start | bytes 7864320 | tf_op jit(solution)/shard_map/all_to_all | solution.py:132
  98.3 3.0 %copy.82 = f32[20,16,24,128]{3,0,2,1:T(8,128)S(1)} copy(f32[20,16,24,128]{3,2,0,1:T(8,128)} %all-to-all-done) | data formatting | bytes 7864320 | tf_op jit(solution)/shard_map/all_to_all | solution.py:132
  101.3 5.1 %fusion.33 = f32[768,20,12]{0,1,2:T(8,128)S(1)} fusion(f32[20,32,12,128]{3,0,2,1:T(8,128)S(1)} %bitcast.154, bf16[768,32,128]{2,0,1:T(8,128)(2,1)} %get-tuple-element.8), kind=kOutput, calls=%fused_computation.52 | convolution fusion | flops 1509949440 | bytes 10960896 | tf_op jit(solution)/shard_map/dot_general | solution.py:76
  106.4 2.2 %fusion.60 = f32[768,20,12]{0,1,2:T(8,128)S(1)} fusion(f32[768,20,12]{0,1,2:T(8,128)S(1)} %fusion.33, f32[20,32,12,128]{3,0,2,1:T(8,128)S(1)} %bitcast.155, bf16[768,32,128]{2,0,1:T(8,128)(2,1)S(1)} %bitcast.148), kind=kOutput, calls=%fused_computation.61 | convolution fusion | flops 1514065920 | bytes 11698176 | tf_op jit(solution)/shard_map/dot_general | solution.py:77
  108.6 2.1 %fusion.54 = f32[768,20,12]{0,1,2:T(8,128)S(1)} fusion(f32[768,20,12]{0,1,2:T(8,128)S(1)} %fusion.60, f32[20,32,12,128]{3,0,2,1:T(8,128)S(1)} %bitcast.156, bf16[768,32,128]{2,0,1:T(8,128)(2,1)S(1)} %bitcast.144), kind=kOutput, calls=%fused_computation.59 | convolution fusion | flops 1510133760 | bytes 11698176 | tf_op jit(solution)/shard_map/dot_general | solution.py:78
  111.0 1.4 reshape.423
  112.5 2.4 %copy.86 = f32[8,96,240]{2,1,0:T(8,128)} copy(f32[8,96,240]{1,0,2:T(8,128)} %reshape.423) | data formatting | bytes 1474560 | tf_op jit(solution)/shard_map/reshape | solution.py:80
  114.9 31.6 %all-to-all-done.2 = f32[20,16,24,128]{3,2,0,1:T(8,128)} async-done(((f32[20,16,24,128]{3,2,0,1:T(8,128)}), f32[20,16,24,128]{3,2,0,1:T(8,128)}, u32[]{:S(2)}, u32[]{:S(2)}) %all-to-all-start.2) | async-done | bytes 3932192 | tf_op jit(solution)/shard_map/all_to_all | solution.py:132
  146.5 10.4 %all-to-all-start.1 = ((f32[8,96,240]{2,1,0:T(8,128)}), f32[8,96,240]{2,1,0:T(8,128)}, u32[]{:S(2)}, u32[]{:S(2)}) async-start(f32[8,96,240]{2,1,0:T(8,128)} %copy.86), calls=%async_computation.1 | async-start | bytes 1572864 | tf_op jit(solution)/shard_map/all_to_all | solution.py:81
  157.0 3.0 %copy.93 = f32[20,16,24,128]{3,0,2,1:T(8,128)S(1)} copy(f32[20,16,24,128]{3,2,0,1:T(8,128)} %all-to-all-done.2) | data formatting | bytes 7864320 | tf_op jit(solution)/shard_map/all_to_all | solution.py:132
  160.0 5.6 %fusion.39 = f32[768,20,12]{0,1,2:T(8,128)S(1)} fusion(f32[20,32,12,128]{3,0,2,1:T(8,128)S(1)} %bitcast.151, bf16[768,32,128]{2,0,1:T(8,128)(2,1)} %get-tuple-element.8), kind=kOutput, calls=%fused_computation.54 | convolution fusion | flops 1509949440 | bytes 10960896 | tf_op jit(solution)/shard_map/dot_general | solution.py:76
  165.6 2.2 %fusion.57 = f32[768,20,12]{0,1,2:T(8,128)S(1)} fusion(f32[768,20,12]{0,1,2:T(8,128)S(1)} %fusion.39, f32[20,32,12,128]{3,0,2,1:T(8,128)S(1)} %bitcast.152, bf16[768,32,128]{2,0,1:T(8,128)(2,1)S(1)} %bitcast.150), kind=kOutput, calls=%fused_computation.60 | convolution fusion | flops 1514065920 | bytes 11698176 | tf_op jit(solution)/shard_map/dot_general | solution.py:77
  167.8 2.2 %fusion.51 = f32[768,20,12]{0,1,2:T(8,128)S(1)} fusion(f32[768,20,12]{0,1,2:T(8,128)S(1)} %fusion.57, f32[20,32,12,128]{3,0,2,1:T(8,128)S(1)} %bitcast.153, bf16[768,32,128]{2,0,1:T(8,128)(2,1)S(1)} %bitcast.146), kind=kOutput, calls=%fused_computation.58 | convolution fusion | flops 1510133760 | bytes 11698176 | tf_op jit(solution)/shard_map/dot_general | solution.py:78
  170.2 1.4 reshape.428
  171.6 2.4 %copy.97 = f32[8,96,240]{2,1,0:T(8,128)} copy(f32[8,96,240]{1,0,2:T(8,128)} %reshape.428) | data formatting | bytes 1474560 | tf_op jit(solution)/shard_map/reshape | solution.py:80
  174.0 4.8 %all-to-all-start.3 = ((f32[8,96,240]{2,1,0:T(8,128)}), f32[8,96,240]{2,1,0:T(8,128)}, u32[]{:S(2)}, u32[]{:S(2)}) async-start(f32[8,96,240]{2,1,0:T(8,128)} %copy.97), calls=%async_computation.3 | async-start | bytes 1572864 | tf_op jit(solution)/shard_map/all_to_all | solution.py:81
  179.6 2.0 convolution_bitcast_fusion.1
  181.6 1.3 reshape.425
  182.9 1.2 copy.89
  184.8 6.3 %all-to-all-done.3 = f32[8,96,240]{2,1,0:T(8,128)} async-done(((f32[8,96,240]{2,1,0:T(8,128)}), f32[8,96,240]{2,1,0:T(8,128)}, u32[]{:S(2)}, u32[]{:S(2)}) %all-to-all-start.3) | async-done | bytes 737312 | tf_op jit(solution)/shard_map/all_to_all | solution.py:81
  191.1 2.0 convolution_bitcast_fusion
  193.1 1.3 reshape.430
  196.4 3.1 %fusion.21 = (f32[3,20,288]{2,1,0:T(8,128)S(1)}, f32[3,20,288]{2,1,0:T(8,128)S(1)}, f32[3,20,288]{2,1,0:T(8,128)S(1)}, f32[3,20,288]{2,1,0:T(8,128)S(1)}) fusion(f32[3,20,288]{2,1,0:T(8,128)S(1)} %get-tuple-element.35, f32[3,20,288]{2,1,0:T(8,128)S(1)} %get-tuple-element.36, bf16[3,20,20,1,1,288]{5,4,3,2,1,0:T(2,128)(2,1)} %get-tuple-element.20, ...), kind=kLoop, calls=%fused_computation.37 | loop fusion | flops 6151680 | bytes 1935360 | tf_op jit(solution)/shard_map/reduce_sum | solution.py:93
  (61 shorter events, 7.8 us)
Async XLA Ops:
  23.8 63.0 %all-to-all-start = ((f32[20,16,24,128]{3,2,0,1:T(8,128)}), f32[20,16,24,128]{3,2,0,1:T(8,128)}, u32[]{:S(2)}, u32[]{:S(2)}) async-start(f32[20,16,24,128]{3,2,0,1:T(8,128)} %copy.81), calls=%async_computation | async-start | bytes 7864320 | tf_op jit(solution)/shard_map/all_to_all | solution.py:132
  33.6 7.9 %copy-start = (f32[20,384,128]{2,1,0:T(8,128)S(1)}, f32[20,384,128]{2,1,0:T(8,128)}, u32[]{:S(2)}) copy-start(f32[20,384,128]{2,1,0:T(8,128)} %get-tuple-element.17) | copy-start | bytes 11796484
  41.5 2.3 %copy-start.1 = (bf16[3,20,20,1,2,288]{5,4,3,2,1,0:T(2,128)(2,1)S(1)}, bf16[3,20,20,1,2,288]{5,4,3,2,1,0:T(2,128)(2,1)}, u32[]{:S(2)}) copy-start(bf16[3,20,20,1,2,288]{5,4,3,2,1,0:T(2,128)(2,1)} %param.3) | copy-start | bytes 4147204
  86.9 59.7 %all-to-all-start.2 = ((f32[20,16,24,128]{3,2,0,1:T(8,128)}), f32[20,16,24,128]{3,2,0,1:T(8,128)}, u32[]{:S(2)}, u32[]{:S(2)}) async-start(f32[20,16,24,128]{3,2,0,1:T(8,128)} %copy.92), calls=%async_computation.2 | async-start | bytes 7864320 | tf_op jit(solution)/shard_map/all_to_all | solution.py:132
  98.2 8.1 %slice-start.4 = ((s8[6291456]{0:T(1024)(128)(4,1)}), s8[4194304]{0:T(1024)(128)(4,1)S(1)}, s32[]{:S(2)}) async-start(s8[6291456]{0:T(1024)(128)(4,1)} %bitcast.147), calls=%async_computation.8 | async-start | bytes 8388608
  101.3 5.1 %slice-start.5 = ((s8[6291456]{0:T(1024)(128)(4,1)}), s8[2097152]{0:T(1024)(128)(4,1)S(1)}, s32[]{:S(2)}) async-start(s8[6291456]{0:T(1024)(128)(4,1)} %bitcast.147), calls=%async_computation.9 | async-start | bytes 4194304
  101.3 7.3 %slice-start = ((s8[6291456]{0:T(1024)(128)(4,1)}), s8[4194304]{0:T(1024)(128)(4,1)S(1)}, s32[]{:S(2)}) async-start(s8[6291456]{0:T(1024)(128)(4,1)} %bitcast.143), calls=%async_computation.4 | async-start | bytes 8388608
  106.4 2.2 %slice-start.1 = ((s8[6291456]{0:T(1024)(128)(4,1)}), s8[2097152]{0:T(1024)(128)(4,1)S(1)}, s32[]{:S(2)}) async-start(s8[6291456]{0:T(1024)(128)(4,1)} %bitcast.143), calls=%async_computation.5 | async-start | bytes 4194304
  146.5 27.5 %all-to-all-start.1 = ((f32[8,96,240]{2,1,0:T(8,128)}), f32[8,96,240]{2,1,0:T(8,128)}, u32[]{:S(2)}, u32[]{:S(2)}) async-start(f32[8,96,240]{2,1,0:T(8,128)} %copy.86), calls=%async_computation.1 | async-start | bytes 1572864 | tf_op jit(solution)/shard_map/all_to_all | solution.py:81
  157.0 8.6 %slice-start.6 = ((s8[6291456]{0:T(1024)(128)(4,1)}), s8[4194304]{0:T(1024)(128)(4,1)S(1)}, s32[]{:S(2)}) async-start(s8[6291456]{0:T(1024)(128)(4,1)} %bitcast.149), calls=%async_computation.10 | async-start | bytes 8388608
  157.0 10.8 %slice-start.2 = ((s8[6291456]{0:T(1024)(128)(4,1)}), s8[4194304]{0:T(1024)(128)(4,1)S(1)}, s32[]{:S(2)}) async-start(s8[6291456]{0:T(1024)(128)(4,1)} %bitcast.145), calls=%async_computation.6 | async-start | bytes 8388608
  160.0 5.6 %slice-start.7 = ((s8[6291456]{0:T(1024)(128)(4,1)}), s8[2097152]{0:T(1024)(128)(4,1)S(1)}, s32[]{:S(2)}) async-start(s8[6291456]{0:T(1024)(128)(4,1)} %bitcast.149), calls=%async_computation.11 | async-start | bytes 4194304
  160.0 7.8 %slice-start.3 = ((s8[6291456]{0:T(1024)(128)(4,1)}), s8[2097152]{0:T(1024)(128)(4,1)S(1)}, s32[]{:S(2)}) async-start(s8[6291456]{0:T(1024)(128)(4,1)} %bitcast.145), calls=%async_computation.7 | async-start | bytes 4194304
  174.0 17.1 %all-to-all-start.3 = ((f32[8,96,240]{2,1,0:T(8,128)}), f32[8,96,240]{2,1,0:T(8,128)}, u32[]{:S(2)}, u32[]{:S(2)}) async-start(f32[8,96,240]{2,1,0:T(8,128)} %copy.97), calls=%async_computation.3 | async-start | bytes 1572864 | tf_op jit(solution)/shard_map/all_to_all | solution.py:81
